TPU v7x, 32 devices: a whole 2x2x4 slice. The times are simulated.
32 devices in a mesh: seq: 8 (over z, y), tp: 4 (over x, core).
Axes of the slice: x: 2, y: 2, z: 4, core: 2. Of those that a mesh axis runs over, the one named last changes fastest.
Arguments:
- layer_activation: bfloat16 [3072, 2048], P('seq', 'tp'), may hold values from -6 to 6
- sequence_label: int32 [3072], P('seq'), may hold values from 0 to 2, as said below
- sequence_extents: int32 [2], replicated, may hold values from 1 to 1920, as said below
- destination_slots: int32 [2], replicated, may hold values from 0 to 7, as said below
- entry_layernorm_coef: float32 [2048], replicated, may hold values from 0.5 to 1.5
- lagged_blend_coefs: float32 [6, 2048], replicated, may hold values from 0 to 1
- query_matrix: bfloat16 [2048, 2048], P(None, 'tp'), may hold values from -0.125 to 0.125
- lookup_matrix: bfloat16 [2048, 2048], P(None, 'tp'), may hold values from -0.125 to 0.125
- content_matrix: bfloat16 [2048, 2048], P(None, 'tp'), may hold values from -0.125 to 0.125
- readout_matrix: bfloat16 [2048, 2048], P('tp'), may hold values from -0.125 to 0.125
- forgetting_narrow_matrix: bfloat16 [2048, 96], replicated, may hold values from -0.125 to 0.125
- forgetting_widen_matrix: bfloat16 [96, 2048], P(None, 'tp'), may hold values from -2.5 to 2.5
- forgetting_offset: float32 [2048], P('tp'), may hold values from -11 to -3.5
- stepsize_narrow_matrix: bfloat16 [2048, 96], replicated, may hold values from -0.125 to 0.125
- stepsize_widen_matrix: bfloat16 [96, 2048], P(None, 'tp'), may hold values from -0.625 to 0.625
- stepsize_offset: float32 [2048], P('tp'), may hold values from -4 to 4
- gating_narrow_matrix: bfloat16 [2048, 256], replicated, may hold values from -0.125 to 0.125
- gating_widen_matrix: bfloat16 [256, 2048], P(None, 'tp'), may hold values from -0.375 to 0.375
- erasure_lookup_coef: float32 [2048], P('tp'), may hold values from 0.5 to 1.5
- lookup_step_fraction: float32 [2048], P('tp'), may hold values from 0 to 1
- diagonal_reward_coef: float32 [2048], P('tp'), may hold values from -3 to 3
- group_layernorm_coef: float32 [2048], P('tp'), may hold values from 0.5 to 1.5
Outputs:
- mixed: bfloat16 [3072, 2048], P('seq', 'tp')
- final_states: float32 [8, 32, 64, 64], P('seq', 'tp')
- final_rows: bfloat16 [8, 2048], P('seq', 'tp')
Inputs may be any that keep to these rules, and one draw needn't show every extreme that they name: `sequence_label`: token p is in prompt 0 for p < sequence_extents[0], in prompt 1 for the next sequence_extents[1] tokens, and padding (2) after them; at least one padding token. `sequence_extents`: one length is exactly 1920, the other at least 768; their sum is under 3072. `destination_slots`: the two owners differ, and one of them is the last index of seq.
All inputs are finite; a program needn't handle non-finite values.
Results may differ from a plain program's by a relative error of at most 0.012.
Values may be sent and summed in bfloat16 or wider, within the bound.
A program may use at most 128 MiB of HBM per device.

v0:
```python
import jax
import jax.numpy as jnp
from jax import lax
from jax.sharding import PartitionSpec as P

CHANNELS_PER_ONE = 64
PROMPTS = 2
EPS = 1e-05
GROUP_EPS = 0.00064


def from_behind(array, axis, by):
    length = lax.axis_size(axis)
    pairs = [(i, i + by) for i in range(length) if 0 <= i + by < length]
    return lax.ppermute(array, axis, pairs)


def broadcast(value, axis, source):
    kept = jnp.where(lax.axis_index(axis) == source, value, 0).astype(value.dtype)
    return lax.psum(kept, axis)


def matmul(left, right):
    return jnp.dot(left, right, preferred_element_type=jnp.float32)


def compose(earlier_map, later_map):
    return jnp.einsum("hij,hjk->hik", earlier_map, later_map, precision=lax.Precision.HIGHEST)


def on_device(
    layer_activation,
    sequence_label,
    sequence_extents,
    destination_slots,
    entry_layernorm_coef,
    lagged_blend_coefs,
    query_matrix,
    lookup_matrix,
    content_matrix,
    readout_matrix,
    forgetting_narrow_matrix,
    forgetting_widen_matrix,
    forgetting_offset,
    stepsize_narrow_matrix,
    stepsize_widen_matrix,
    stepsize_offset,
    gating_narrow_matrix,
    gating_widen_matrix,
    erasure_lookup_coef,
    lookup_step_fraction,
    diagonal_reward_coef,
    group_layernorm_coef,
):
    highest = lax.Precision.HIGHEST
    segment_length = layer_activation.shape[0]
    stepsize_fraction = query_matrix.shape[1]
    local_attentioners = stepsize_fraction // CHANNELS_PER_ONE
    position = lax.axis_index("seq")
    column = lax.axis_index("tp")
    gathered = lax.all_gather(layer_activation, "tp", axis=1, tiled=True)
    floats = gathered.astype(jnp.float32)
    average = jnp.mean(floats, axis=1, keepdims=True)
    centred = floats - average
    variance = jnp.mean(centred * centred, axis=1, keepdims=True)
    normed = (centred * lax.rsqrt(variance + EPS) * entry_layernorm_coef).astype(jnp.bfloat16)
    normal_f = normed.astype(jnp.float32)
    arrived = from_behind(normed[-1:], "seq", 1)
    bounds = jnp.cumsum(sequence_extents)
    first_token = position * segment_length
    before = first_token - 1
    segment_before = (before >= bounds[0]).astype(jnp.int32) + (before >= bounds[1]).astype(
        jnp.int32
    )
    joined = (segment_before == sequence_label[0]) & (position > 0)
    continues = jnp.concatenate([joined[None], sequence_label[1:] == sequence_label[:-1]])
    previous = jnp.concatenate([arrived.astype(jnp.float32), normal_f[:-1]], axis=0)
    previous = jnp.where(continues[:, None], previous, jnp.zeros_like(previous))
    difference = previous - normal_f

    def blended(which):
        return (normal_f + difference * lagged_blend_coefs[which]).astype(jnp.bfloat16)

    receptance = matmul(blended(0), query_matrix)
    keys = matmul(blended(2), lookup_matrix)
    values = matmul(blended(3), content_matrix)
    decay_hidden = jnp.tanh(matmul(blended(1), forgetting_narrow_matrix)).astype(jnp.bfloat16)
    learn_hidden = matmul(blended(4), stepsize_narrow_matrix).astype(jnp.bfloat16)
    gate_hidden = jax.nn.sigmoid(matmul(blended(5), gating_narrow_matrix)).astype(jnp.bfloat16)
    log_rate = (
        -jax.nn.softplus(-(forgetting_offset + matmul(decay_hidden, forgetting_widen_matrix))) - 0.5
    )
    log_decay = -jnp.exp(log_rate)
    learning = jax.nn.sigmoid(stepsize_offset + matmul(learn_hidden, stepsize_widen_matrix))
    gating_signal = matmul(gate_hidden, gating_widen_matrix)
    removal = (keys * erasure_lookup_coef).reshape(
        segment_length, local_attentioners, CHANNELS_PER_ONE
    )
    removal = removal * lax.rsqrt(jnp.sum(removal * removal, axis=-1, keepdims=True) + 1e-06)
    written = keys * (1.0 + (learning - 1.0) * lookup_step_fraction)
    split_queries = receptance.reshape(segment_length, local_attentioners, CHANNELS_PER_ONE)
    split_lookups = written.reshape(segment_length, local_attentioners, CHANNELS_PER_ONE)
    split_contents = values.reshape(segment_length, local_attentioners, CHANNELS_PER_ONE)
    head_w = log_decay.reshape(segment_length, local_attentioners, CHANNELS_PER_ONE)
    head_a = learning.reshape(segment_length, local_attentioners, CHANNELS_PER_ONE)
    padded_v = jnp.concatenate([split_contents, jnp.zeros_like(split_contents)], axis=-1)
    local_ends = bounds - 1 - first_token
    block_len = min(64, segment_length)
    blocks = segment_length // block_len
    steps_in = jnp.arange(block_len, dtype=jnp.int32)
    strict_lower = steps_in[:, None] > steps_in[None, :]
    with_diag = steps_in[:, None] >= steps_in[None, :]
    unit_eye = jnp.eye(block_len, dtype=jnp.float32)

    def regroup(array):
        return array.reshape((blocks, block_len) + array.shape[1:])

    def block_step(carry, inputs):
        stacked, saved = carry
        block_start, still, r_blk, k_blk, v_blk, n_blk, lw_blk, a_blk = inputs
        restarts = jnp.logical_not(still).astype(jnp.int32)
        epochs = jnp.cumsum(restarts)
        from_start = (epochs == 0).astype(jnp.float32)
        log_total = jnp.cumsum(lw_blk, axis=0)
        query_a = -n_blk * jnp.exp(log_total - lw_blk)
        scaled_beta = n_blk * a_blk * jnp.exp(-log_total)
        scaled_key = k_blk * jnp.exp(-log_total)
        scaled_query = r_blk * jnp.exp(log_total)
        same_run = epochs[:, None] == epochs[None, :]
        strict_mask = (strict_lower & same_run).astype(jnp.float32)
        diag_mask = (with_diag & same_run).astype(jnp.float32)

        def paired(left, right, mask):
            return jnp.einsum("thj,shj->hts", left, right, precision=highest) * mask[None]

        mix_beta = paired(query_a, scaled_beta, strict_mask)
        mix_key = paired(query_a, scaled_key, strict_mask)
        read_beta = paired(scaled_query, scaled_beta, diag_mask)
        read_key = paired(scaled_query, scaled_key, diag_mask)
        from_state = jnp.einsum(
            "thj,hij->hti", query_a * from_start[:, None, None], stacked, precision=highest
        )
        right_side = from_state + jnp.einsum("hts,shi->hti", mix_key, v_blk, precision=highest)
        pseudo = jax.scipy.linalg.solve_triangular(
            unit_eye[None] - mix_beta, right_side, lower=True, unit_diagonal=True
        )
        outputs_blk = jnp.einsum(
            "thj,hij->thi", scaled_query * from_start[:, None, None], stacked, precision=highest
        )
        outputs_blk = outputs_blk + jnp.einsum("hts,hsi->thi", read_beta, pseudo, precision=highest)
        outputs_blk = outputs_blk + jnp.einsum("hts,shi->thi", read_key, v_blk, precision=highest)

        def state_at(moment):
            growth = jnp.exp(lax.dynamic_index_in_dim(log_total, moment, 0, keepdims=False))
            epoch_now = lax.dynamic_index_in_dim(epochs, moment, 0, keepdims=False)
            chosen = ((steps_in <= moment) & (epochs == epoch_now)).astype(jnp.float32)
            weight_beta = scaled_beta * chosen[:, None, None] * growth[None]
            weight_key = scaled_key * chosen[:, None, None] * growth[None]
            start_part = stacked * (growth * (epoch_now == 0).astype(jnp.float32))[:, None, :]
            result = start_part + jnp.einsum("hsi,shj->hij", pseudo, weight_beta, precision=highest)
            return result + jnp.einsum("shi,shj->hij", v_blk, weight_key, precision=highest)

        new_stacked = state_at(jnp.int32(block_len - 1))
        updated = []
        for prompt in range(PROMPTS):
            offset_end = local_ends[prompt] - block_start
            inside = (offset_end >= 0) & (offset_end < block_len)
            moment = jnp.clip(offset_end, 0, block_len - 1)
            updated.append(jnp.where(inside, state_at(moment), saved[prompt]))
        return ((new_stacked, jnp.stack(updated)), outputs_blk)

    identity = jnp.broadcast_to(
        jnp.eye(CHANNELS_PER_ONE, dtype=jnp.float32),
        (local_attentioners, CHANNELS_PER_ONE, CHANNELS_PER_ONE),
    )
    start_stack = jnp.concatenate([jnp.zeros_like(identity), identity], axis=1)
    start_saved = jnp.zeros(
        (PROMPTS, local_attentioners, 2 * CHANNELS_PER_ONE, CHANNELS_PER_ONE), jnp.float32
    )
    block_starts = jnp.arange(blocks, dtype=jnp.int32) * block_len
    scan_inputs = (
        block_starts,
        regroup(continues),
        regroup(split_queries),
        regroup(split_lookups),
        regroup(padded_v),
        regroup(removal),
        regroup(head_w),
        regroup(head_a),
    )
    (final_stack, saved), grouped_out = lax.scan(
        block_step, (start_stack, start_saved), scan_inputs
    )
    outputs = grouped_out.reshape(segment_length, local_attentioners, 2 * CHANNELS_PER_ONE)
    local_state = final_stack[:, :CHANNELS_PER_ONE]
    transition = final_stack[:, CHANNELS_PER_ONE:]

    def passing(turn, incoming):
        return from_behind(
            (compose(incoming, transition) + local_state).astype(jnp.bfloat16), "seq", 1
        ).astype(jnp.float32)

    state_in = lax.fori_loop(0, lax.axis_size("seq") - 1, passing, jnp.zeros_like(local_state))
    readout = outputs[:, :, :CHANNELS_PER_ONE] + jnp.einsum(
        "hij,thj->thi", state_in, outputs[:, :, CHANNELS_PER_ONE:], precision=highest
    )
    centre = readout - jnp.mean(readout, axis=-1, keepdims=True)
    spread = jnp.mean(centre * centre, axis=-1, keepdims=True)
    group_standardized = (
        centre
        * lax.rsqrt(spread + GROUP_EPS)
        * group_layernorm_coef.reshape(local_attentioners, CHANNELS_PER_ONE)
    )
    diagonal_reward = (
        jnp.sum(
            split_queries
            * split_lookups
            * diagonal_reward_coef.reshape(local_attentioners, CHANNELS_PER_ONE),
            axis=-1,
            keepdims=True,
        )
        * split_contents
    )
    visible_entries = (
        (group_standardized + diagonal_reward).reshape(segment_length, stepsize_fraction)
        * gating_signal
    ).astype(jnp.bfloat16)
    partial_value = matmul(visible_entries, readout_matrix)
    summed = lax.psum_scatter(
        partial_value.astype(jnp.bfloat16), "tp", scatter_dimension=1, tiled=True
    ).astype(jnp.float32)
    mixed = (summed + layer_activation.astype(jnp.float32)).astype(jnp.bfloat16)
    final_states = jnp.zeros(
        (1, local_attentioners, CHANNELS_PER_ONE, CHANNELS_PER_ONE), jnp.float32
    )
    final_rows = jnp.zeros((1, stepsize_fraction), jnp.bfloat16)
    for prompt in range(PROMPTS):
        last_token = bounds[prompt] - 1
        holder = last_token // segment_length
        inside = jnp.clip(last_token - first_token, 0, segment_length - 1)
        recorded = saved[prompt]
        state_end = (
            compose(state_in, recorded[:, CHANNELS_PER_ONE:]) + recorded[:, :CHANNELS_PER_ONE]
        )
        row_end = lax.dynamic_slice(
            normal_f, (inside, column * stepsize_fraction), (1, stepsize_fraction)
        )
        got_state, got_row = (
            broadcast(state_end.astype(jnp.bfloat16), "seq", holder).astype(state_end.dtype),
            broadcast(row_end.astype(jnp.bfloat16), "seq", holder).astype(row_end.dtype),
        )
        is_owner = position == destination_slots[prompt]
        final_states = jnp.where(is_owner, got_state[None], final_states)
        final_rows = jnp.where(is_owner, got_row.astype(jnp.bfloat16), final_rows)
    return (mixed, final_states, final_rows)


def solution(mesh):
    return jax.shard_map(
        on_device,
        mesh=mesh,
        in_specs=(
            P("seq", "tp"),
            P("seq"),
            P(),
            P(),
            P(),
            P(),
            P(None, "tp"),
            P(None, "tp"),
            P(None, "tp"),
            P("tp", None),
            P(),
            P(None, "tp"),
            P("tp"),
            P(),
            P(None, "tp"),
            P("tp"),
            P(),
            P(None, "tp"),
            P("tp"),
            P("tp"),
            P("tp"),
            P("tp"),
        ),
        out_specs=(P("seq", "tp"), P("seq", "tp", None, None), P("seq", "tp")),
        check_vma=False,
    )
```

profile of v0, /device:TPU:0, one launch (start us, length us, event | category | flops | bytes accessed | tf_op | source)
XLA Modules:
  0.0 698.0 jit_solution(5239069506846674704)
XLA Ops:
  14.6 17.4 %all-gather.2.cloned.1.call-done = bf16[384,2048]{1,0:T(8,128)(2,1)} async-done(((bf16[384,512]{1,0:T(8,128)(2,1)}), bf16[384,2048]{1,0:T(8,128)(2,1)}) %all-gather.2.cloned.1.call-update) | async-done | bytes 1572880 | tf_op jit(solution)/shard_map/all_gather | solution.py:61
  32.0 1.8 convert_reduce_fusion
  33.8 2.0 fusion.61
  37.5 3.4 collective-permute-start.1
  42.8 3.5 slice.133
  46.3 3.9 fusion.101
  51.7 5.1 fusion.72
  56.7 2.5 reshape_reshape.15
  59.3 5.5 fusion.149
  66.4 2.3 copy.125
  68.7 5.1 fusion.139
  73.8 2.7 reshape_reshape.12
  76.5 2.6 reshape.279
  80.6 4.5 fusion.74
  86.8 2.8 concatenate.15.clone
  89.6 1.7 broadcast_multiply_fusion.2
  92.1 414.9 %while.27 = (s32[]{:T(128)}, f32[8,128,64]{1,2,0:T(8,128)S(1)}, f32[2,8,128,64]{2,3,1,0:T(8,128)}, f32[6,64,8,128]{3,2,1,0:T(8,128)}, f32[6,64,8,64]{3,2,1,0:T(8...) while((s32[]{:T(128)}, f32[8,128,64]{1,2,0:T(8,128)S(1)}, ...), condition=%wide.region_7.8_spmd.clone.clone, body=%wide.region_4.7_spmd.clone.clone.sunk | while | flops 708762112 | bytes 20262212 | solution.py:191
  99.0 2.0 and_convert_fusion.4
  103.1 2.4 multiply_multiply_fusion.8
  108.9 40.7 %custom-call.9 = f32[8,1,64,64]{2,3,1,0:T(8,128)} custom-call(f32[8,1,64,64]{3,2,1,0:T(8,128)} %fusion.259), custom_call_target="InvertDiagBlocksLowerTriangular" | custom-call | tf_op jit(solution)/shard_map/while/body/eval_jaxpr/jit(_solve_triangular)/vmap()/triangular_solve | solution.py:144
  149.6 1.7 fusion.260
  168.1 2.0 and_convert_fusion.4
  172.3 2.4 multiply_multiply_fusion.8
  178.1 40.7 %custom-call.9 = f32[8,1,64,64]{2,3,1,0:T(8,128)} custom-call(f32[8,1,64,64]{3,2,1,0:T(8,128)} %fusion.259), custom_call_target="InvertDiagBlocksLowerTriangular" | custom-call | tf_op jit(solution)/shard_map/while/body/eval_jaxpr/jit(_solve_triangular)/vmap()/triangular_solve | solution.py:144
  237.3 2.0 and_convert_fusion.4
  241.4 2.4 multiply_multiply_fusion.8
  247.2 40.7 %custom-call.9 = f32[8,1,64,64]{2,3,1,0:T(8,128)} custom-call(f32[8,1,64,64]{3,2,1,0:T(8,128)} %fusion.259), custom_call_target="InvertDiagBlocksLowerTriangular" | custom-call | tf_op jit(solution)/shard_map/while/body/eval_jaxpr/jit(_solve_triangular)/vmap()/triangular_solve | solution.py:144
  306.4 2.0 and_convert_fusion.4
  310.6 2.4 multiply_multiply_fusion.8
  316.4 40.7 %custom-call.9 = f32[8,1,64,64]{2,3,1,0:T(8,128)} custom-call(f32[8,1,64,64]{3,2,1,0:T(8,128)} %fusion.259), custom_call_target="InvertDiagBlocksLowerTriangular" | custom-call | tf_op jit(solution)/shard_map/while/body/eval_jaxpr/jit(_solve_triangular)/vmap()/triangular_solve | solution.py:144
  375.6 2.0 and_convert_fusion.4
  379.8 2.4 multiply_multiply_fusion.8
  385.5 40.7 %custom-call.9 = f32[8,1,64,64]{2,3,1,0:T(8,128)} custom-call(f32[8,1,64,64]{3,2,1,0:T(8,128)} %fusion.259), custom_call_target="InvertDiagBlocksLowerTriangular" | custom-call | tf_op jit(solution)/shard_map/while/body/eval_jaxpr/jit(_solve_triangular)/vmap()/triangular_solve | solution.py:144
  444.8 2.0 and_convert_fusion.4
  448.9 2.4 multiply_multiply_fusion.8
  454.7 40.7 %custom-call.9 = f32[8,1,64,64]{2,3,1,0:T(8,128)} custom-call(f32[8,1,64,64]{3,2,1,0:T(8,128)} %fusion.259), custom_call_target="InvertDiagBlocksLowerTriangular" | custom-call | tf_op jit(solution)/shard_map/while/body/eval_jaxpr/jit(_solve_triangular)/vmap()/triangular_solve | solution.py:144
  495.4 1.7 fusion.260
  507.3 2.4 copy.127
  509.7 2.4 slice_bitcast_fusion.1
  512.1 2.1 fusion.152
  514.2 2.8 copy.135
  517.1 55.1 %while.28 = (s32[]{:T(128)}, f32[8,64,64]{2,1,0:T(8,128)S(1)}, f32[8,64,64]{2,1,0:T(8,128)S(1)}, f32[8,64,64]{2,1,0:T(8,128)S(1)}, s32[]{:T(128)}, /*index=5*/s32[]{:T(128)}) while((s32[]{:T(128)}, f32[8,64,64]{2,1,0:T(8,128)S(1)}, f32[8,64,64]{2,1,0:T(8,128)S(1)}, f32[8,64,64]{2,1,0:T(8,128)S(1)}, s32[]{:T(128)}, ...), condition=%wide.region_9.10_spmd.clone, body=%wide.region_8.9_spmd.clone.sunk | while | flops 25296900 | bytes 917623 | solution.py:203
  517.4 3.4 collective-permute-start
  520.8 2.8 collective-permute-done
  524.1 4.4 collective-permute-start
  528.5 2.5 collective-permute-done
  531.4 4.4 collective-permute-start
  535.8 2.5 collective-permute-done
  538.7 5.2 collective-permute-start
  543.9 2.5 collective-permute-done
  546.9 5.3 collective-permute-start
  552.1 2.5 collective-permute-done
  555.1 5.3 collective-permute-start
  560.3 3.0 collective-permute-done
  563.8 5.6 collective-permute-start
  569.4 2.5 collective-permute-done
  572.1 4.1 fusion.157
  579.0 4.4 fusion.116
  585.6 4.1 convolution_convert_fusion
  592.5 22.7 %all-reduce.2 = (bf16[1,512]{1,0:T(2,128)(2,1)S(1)}, bf16[1,512]{1,0:T(2,128)(2,1)S(1)}) all-reduce(bf16[1,512]{1,0:T(2,128)(2,1)S(1)} %get-tuple-element.333, bf16[1,512]{1,0:T(2,128)(2,1)S(1)} %get-tuple-element.332), channel_id=1, replica_groups=mesh['seq'=8,'tp'=4] {'seq'}, use_global_device_ids=true, to_apply=%region_16.17 | all-reduce | flops 1024 | bytes 4096 | tf_op jit(solution)/shard_map/psum | solution.py:20
  615.9 43.6 %all-reduce.6.cloned.1.call-done = (bf16[8,64,64]{2,1,0:T(8,128)(2,1)}, bf16[8,64,64]{2,1,0:T(8,128)(2,1)}) async-done(((bf16[8,64,64]{2,1,0:T(8,128)(2,1)}, bf16[8,64,64]{2,1,0:T(8,128)(2,1)}), (bf16[8,64,64]{2,1,0:T(8,128)(2,1)}, bf16[8,64,64]{2,1,0:T(8,128)(2,1)})) %all-reduce.6.cloned.1.call-update) | async-done | bytes 131088 | tf_op jit(solution)/shard_map/psum | solution.py:20
  659.4 1.7 select_bitcast_fusion
  661.1 28.5 %reduce-scatter.2.cloned.1.call-done = bf16[384,512]{1,0:T(8,128)(2,1)} async-done(((bf16[384,2048]{1,0:T(8,128)(2,1)}), bf16[384,512]{1,0:T(8,128)(2,1)}) %reduce-scatter.2.cloned.1.call-update) | async-done | bytes 393232 | tf_op jit(solution)/shard_map/reduce_scatter | solution.py:229
  689.6 1.8 add_convert_fusion
  (320 shorter events, 137.1 us)
Async XLA Ops:
  7.2 52.1 %copy-start = (bf16[2048,512]{1,0:T(8,128)(2,1)S(1)}, bf16[2048,512]{1,0:T(8,128)(2,1)}, u32[]{:S(2)}) copy-start(bf16[2048,512]{1,0:T(8,128)(2,1)} %param.33) | copy-start | bytes 6291460
  7.2 28.6 %copy-start.15 = (f32[2048]{0:T(1024)S(1)}, f32[2048]{0:T(1024)}, u32[]{:S(2)}) copy-start(f32[2048]{0:T(1024)} %param.30) | copy-start | bytes 24580
  7.2 24.8 %all-gather.2.cloned.1.call-start = ((), (), s32[]{:S(2)}) async-start(), calls=%async_computation.1 | async-start | bytes 1966080 | tf_op jit(solution)/shard_map/all_gather | solution.py:61
  7.9 651.5 %all-reduce.6.cloned.1.call-start = ((), (), s32[]{:S(2)}) async-start(), calls=%async_computation.3 | async-start | bytes 524288 | tf_op jit(solution)/shard_map/psum | solution.py:20
  14.6 27.9 %copy-start.16 = (f32[512]{0:T(512)S(1)}, f32[512]{0:T(512)}, u32[]{:S(2)}) copy-start(f32[512]{0:T(512)} %param.46) | copy-start | bytes 6148
  14.6 28.0 %copy-start.17 = (f32[512]{0:T(512)S(1)}, f32[512]{0:T(512)}, u32[]{:S(2)}) copy-start(f32[512]{0:T(512)} %param.47) | copy-start | bytes 6148
  32.0 3.8 copy-start.5
  36.3 1.2 copy-start.4
  37.5 8.7 %collective-permute-start.1 = (bf16[1,2048]{1,0:T(2,128)(2,1)S(1)}, bf16[1,2048]{1,0:T(2,128)(2,1)S(1)}, u32[]{:S(2)}, u32[]{:S(2)}) collective-permute-start(bf16[1,2048]{1,0:T(2,128)(2,1)S(1)} %slice.132), channel_id=1, source_target_pairs={{0,4},{4,8},{8,12},{12,16},{16,20},{20,24},{24,28},{1,5},{5,9},{9,... | collective-permute-start | bytes 12296 | tf_op jit(solution)/shard_map/ppermute | solution.py:15
  42.8 3.5 copy-start.19
  42.8 3.5 copy-start.20
  51.7 7.6 %copy-start.21 = (f32[512]{0:T(512)S(1)}, f32[512]{0:T(512)}, u32[]{:S(2)}) copy-start(f32[512]{0:T(512)} %param.44) | copy-start | bytes 6148
  51.7 7.6 %copy-start.22 = (f32[512]{0:T(512)S(1)}, f32[512]{0:T(512)}, u32[]{:S(2)}) copy-start(f32[512]{0:T(512)} %param.45) | copy-start | bytes 6148
  64.8 3.9 copy-start.23
  73.8 5.3 copy-start.14
  85.1 6.1 copy-start.9
  86.8 2.8 copy-start.7
  149.6 4.9 copy-start.1
  155.5 2.8 copy-start.2
  218.7 4.9 copy-start.1
  224.6 2.8 copy-start.2
  287.9 4.9 copy-start.1
  293.8 2.8 copy-start.2
  357.1 4.9 copy-start.1
  363.0 2.8 copy-start.2
  426.2 4.9 copy-start.1
  432.1 2.8 copy-start.2
  495.4 4.9 copy-start.1
  501.3 2.8 copy-start.2
  509.7 2.4 copy-start.6
  512.1 4.9 copy-start.3
  517.4 6.2 collective-permute-start
  524.1 6.9 collective-permute-start
  531.4 6.9 collective-permute-start
  538.7 7.7 %collective-permute-start = (bf16[8,64,64]{2,1,0:T(8,128)(2,1)S(1)}, bf16[8,64,64]{2,1,0:T(8,128)(2,1)S(1)}, u32[]{:S(2)}, u32[]{:S(2)}) collective-permute-start(bf16[8,64,64]{2,1,0:T(8,128)(2,1)S(1)} %fusion.267), channel_id=1, source_target_pairs={{0,4},{4,8},{8,12},{12,16},{16,20},{20,24},{24,28},{1,5},{5,9},{9,... | collective-permute-start | bytes 196616 | tf_op jit(solution)/shard_map/while/body/eval_jaxpr/ppermute | solution.py:15
  546.9 7.8 %collective-permute-start = (bf16[8,64,64]{2,1,0:T(8,128)(2,1)S(1)}, bf16[8,64,64]{2,1,0:T(8,128)(2,1)S(1)}, u32[]{:S(2)}, u32[]{:S(2)}) collective-permute-start(bf16[8,64,64]{2,1,0:T(8,128)(2,1)S(1)} %fusion.267), channel_id=1, source_target_pairs={{0,4},{4,8},{8,12},{12,16},{16,20},{20,24},{24,28},{1,5},{5,9},{9,... | collective-permute-start | bytes 196616 | tf_op jit(solution)/shard_map/while/body/eval_jaxpr/ppermute | solution.py:15
  555.1 8.3 %collective-permute-start = (bf16[8,64,64]{2,1,0:T(8,128)(2,1)S(1)}, bf16[8,64,64]{2,1,0:T(8,128)(2,1)S(1)}, u32[]{:S(2)}, u32[]{:S(2)}) collective-permute-start(bf16[8,64,64]{2,1,0:T(8,128)(2,1)S(1)} %fusion.267), channel_id=1, source_target_pairs={{0,4},{4,8},{8,12},{12,16},{16,20},{20,24},{24,28},{1,5},{5,9},{9,... | collective-permute-start | bytes 196616 | tf_op jit(solution)/shard_map/while/body/eval_jaxpr/ppermute | solution.py:15
  563.8 8.1 %collective-permute-start = (bf16[8,64,64]{2,1,0:T(8,128)(2,1)S(1)}, bf16[8,64,64]{2,1,0:T(8,128)(2,1)S(1)}, u32[]{:S(2)}, u32[]{:S(2)}) collective-permute-start(bf16[8,64,64]{2,1,0:T(8,128)(2,1)S(1)} %fusion.267), channel_id=1, source_target_pairs={{0,4},{4,8},{8,12},{12,16},{16,20},{20,24},{24,28},{1,5},{5,9},{9,... | collective-permute-start | bytes 196616 | tf_op jit(solution)/shard_map/while/body/eval_jaxpr/ppermute | solution.py:15
  572.1 4.3 copy-start.8
  572.1 4.3 copy-start.10
  579.0 4.4 copy-start.13
  579.0 5.5 copy-start.12
  585.6 4.2 copy-start.18
  585.6 104.1 %copy-start.11 = (bf16[384,512]{1,0:T(8,128)(2,1)S(1)}, bf16[384,512]{1,0:T(8,128)(2,1)}, u32[]{:S(2)}) copy-start(bf16[384,512]{1,0:T(8,128)(2,1)} %param.26) | copy-start | bytes 1179652
  585.6 104.0 %reduce-scatter.2.cloned.1.call-start = ((), (), s32[]{:S(2)}) async-start(), calls=%async_computation.2 | async-start | bytes 1966080 | tf_op jit(solution)/shard_map/reduce_scatter | solution.py:229
Sparse Core Ops, SparseCore 0:
  9.6 22.3 all-gather.1
  585.7 73.6 all-reduce.5
  662.1 27.4 reduce-scatter.1
where the time goes:
time: 701 us; the launch traced here: 698 us
  other arithmetic  299 us (43%)
  matrix products  120 us (17%)
  waiting for transfers between devices  109 us (16%)
  local copies, waits for them, and re-layouts  62.6 us (9%)
  starting transfers between devices  36.9 us (5%)
  loops' own time  29.5 us (4%)
  blocking collectives  22.7 us (3%)
  between operations  18.8 us (3%)
    another operation x18, other arithmetic, block_step(): jax.scipy.linalg.solve_triangular(unit_eye[None] - mix_beta, right_side,...  245 us
    psum x1, waiting for transfers between devices, broadcast(): return lax.psum(kept, axis)  43.6 us
    ppermute x8, starting transfers between devices, from_behind(): return lax.ppermute(array, axis, pairs)  36.8 us
    dot_general x7, matrix products, matmul(): return jnp.dot(left, right, preferred_element_type=jnp.float32)  32.6 us
    another operation x1, loops' own time, on_device(): lax.scan(block_step, (start_stack, start_saved), scan_inputs)  29.1 us
    reduce_scatter x1, waiting for transfers between devices, on_device(): lax.psum_scatter(partial_value.astype(jnp.bfloat16), 'tp', scatter_dimens...  28.5 us
    psum x1, blocking collectives, broadcast(): return lax.psum(kept, axis)  22.7 us
    dot_general x24, matrix products, paired(): jnp.einsum('thj,shj->hts', left, right, precision=highest) * mask[None]  18.6 us
  transfers between devices with their start and end apart: 11, of which 10 were waited for; matrix products, arithmetic and copies ran while one was open for 2% of the time, Pallas kernels for 0%

commit v1 on v0

--- a/solution.py
+++ b/solution.py
@@ -7,6 +7,16 @@
 PROMPTS = 2
 EPS = 1e-05
 GROUP_EPS = 0.00064
+
+
+def around_the_ring(value, axis, along):
+    count = lax.axis_size(axis)
+    held, blocks = (value, [value])
+    for _ in range(count - 1):
+        held = lax.ppermute(held, axis, [(i, (i + 1) % count) for i in range(count)])
+        blocks.insert(0, held)
+    line = jnp.concatenate(blocks, axis=along)
+    return jnp.roll(line, (lax.axis_index(axis) + 1) * value.shape[along], axis=along)
 
 
 def from_behind(array, axis, by):
@@ -58,7 +68,7 @@
     local_attentioners = stepsize_fraction // CHANNELS_PER_ONE
     position = lax.axis_index("seq")
     column = lax.axis_index("tp")
-    gathered = lax.all_gather(layer_activation, "tp", axis=1, tiled=True)
+    gathered = around_the_ring(layer_activation, "tp", 1)
     floats = gathered.astype(jnp.float32)
     average = jnp.mean(floats, axis=1, keepdims=True)
     centred = floats - average

time: 701 us -> 671 us (0.957)
  waiting for transfers between devices: 109 us -> 78.4 us
    reduce_scatter x1, waiting for transfers between devices: 28.5 us -> 0.01 us  [on_device(): lax.psum_scatter(partial_value.astype(jnp.bfloat16), 'tp', scatter_dimens...]
    all_gather x1 -> x0, waiting for transfers between devices: 17.4 us -> none  [on_device(): gathered = lax.all_gather(layer_activation, 'tp', axis=1, tiled=True)]
    ppermute x0 -> x3, waiting for transfers between devices: none -> 14.7 us  [around_the_ring(): lax.ppermute(held, axis, [(i, (i + 1) % count) for i in range(count)])]
  transfers between devices with their start and end apart: 11 -> 13, of which waited for: 10 -> 11; matrix products, arithmetic and copies ran while one was open for 2% -> 3% of each run, Pallas kernels for 0% -> 0%
where the time goes in v1:
time: 671 us; the launch traced here: 668 us
  other arithmetic  296 us (44%)
  matrix products  120 us (18%)
  waiting for transfers between devices  78.4 us (12%)
  local copies, waits for them, and re-layouts  64 us (10%)
  starting transfers between devices  38.3 us (6%)
  loops' own time  28.1 us (4%)
  blocking collectives  22.9 us (3%)
  between operations  20.6 us (3%)
    another operation x18, other arithmetic, block_step(): jax.scipy.linalg.solve_triangular(unit_eye[None] - mix_beta, right_side,...  245 us
    psum x1, waiting for transfers between devices, broadcast(): return lax.psum(kept, axis)  44.5 us
    ppermute x8, starting transfers between devices, from_behind(): return lax.ppermute(array, axis, pairs)  37.5 us
    dot_general x7, matrix products, matmul(): return jnp.dot(left, right, preferred_element_type=jnp.float32)  32.6 us
    another operation x1, loops' own time, on_device(): lax.scan(block_step, (start_stack, start_saved), scan_inputs)  27.6 us
    psum x1, blocking collectives, broadcast(): return lax.psum(kept, axis)  22.9 us
    ppermute x8, waiting for transfers between devices, from_behind(): return lax.ppermute(array, axis, pairs)  19.1 us
    dot_general x24, matrix products, paired(): jnp.einsum('thj,shj->hts', left, right, precision=highest) * mask[None]  18.6 us
  transfers between devices with their start and end apart: 13, of which 11 were waited for; matrix products, arithmetic and copies ran while one was open for 3% of the time, Pallas kernels for 0%

profile of v1, /device:TPU:0, one launch (start us, length us, event | category | flops | bytes accessed | tf_op | source)
XLA Modules:
  0.0 668.5 jit_solution(13469214140270125074)
XLA Ops:
  13.7 2.5 collective-permute-done.1
  17.2 6.2 collective-permute-done.2
  24.5 6.1 collective-permute-done.3
  34.6 4.4 collective-permute-start.4
  41.5 3.4 slice.133
  45.0 3.9 fusion.101
  50.4 5.1 fusion.72
  55.5 2.5 reshape_reshape.15
  58.0 5.5 fusion.149
  65.2 2.3 copy.125
  67.5 5.1 fusion.139
  72.6 2.7 reshape_reshape.12
  75.4 2.6 reshape.279
  79.4 4.5 fusion.74
  85.6 2.8 concatenate.22.clone
  88.4 1.7 broadcast_multiply_fusion.2
  91.0 412.5 %while.27 = (s32[]{:T(128)}, f32[8,128,64]{1,2,0:T(8,128)S(1)}, f32[2,8,128,64]{2,3,1,0:T(8,128)}, f32[6,64,8,128]{3,2,1,0:T(8,128)}, f32[6,64,8,64]{3,2,1,0:T(8...) while((s32[]{:T(128)}, f32[8,128,64]{1,2,0:T(8,128)S(1)}, ...), condition=%wide.region_7.8_spmd.clone.clone, body=%wide.region_4.7_spmd.clone.clone.sunk | while | flops 708762112 | bytes 20262212 | solution.py:201
  97.4 1.9 and_convert_fusion.4
  101.5 2.4 multiply_multiply_fusion.8
  107.3 40.7 %custom-call.11 = f32[8,1,64,64]{2,3,1,0:T(8,128)} custom-call(f32[8,1,64,64]{3,2,1,0:T(8,128)} %fusion.259), custom_call_target="InvertDiagBlocksLowerTriangular" | custom-call | tf_op jit(solution)/shard_map/while/body/eval_jaxpr/jit(_solve_triangular)/vmap()/triangular_solve | solution.py:154
  166.2 1.9 and_convert_fusion.4
  170.2 2.4 multiply_multiply_fusion.8
  176.1 40.7 %custom-call.11 = f32[8,1,64,64]{2,3,1,0:T(8,128)} custom-call(f32[8,1,64,64]{3,2,1,0:T(8,128)} %fusion.259), custom_call_target="InvertDiagBlocksLowerTriangular" | custom-call | tf_op jit(solution)/shard_map/while/body/eval_jaxpr/jit(_solve_triangular)/vmap()/triangular_solve | solution.py:154
  234.9 1.9 and_convert_fusion.4
  239.0 2.4 multiply_multiply_fusion.8
  244.8 40.7 %custom-call.11 = f32[8,1,64,64]{2,3,1,0:T(8,128)} custom-call(f32[8,1,64,64]{3,2,1,0:T(8,128)} %fusion.259), custom_call_target="InvertDiagBlocksLowerTriangular" | custom-call | tf_op jit(solution)/shard_map/while/body/eval_jaxpr/jit(_solve_triangular)/vmap()/triangular_solve | solution.py:154
  285.5 1.7 fusion.260
  303.7 1.9 and_convert_fusion.4
  307.7 2.4 multiply_multiply_fusion.8
  313.5 40.7 %custom-call.11 = f32[8,1,64,64]{2,3,1,0:T(8,128)} custom-call(f32[8,1,64,64]{3,2,1,0:T(8,128)} %fusion.259), custom_call_target="InvertDiagBlocksLowerTriangular" | custom-call | tf_op jit(solution)/shard_map/while/body/eval_jaxpr/jit(_solve_triangular)/vmap()/triangular_solve | solution.py:154
  354.2 1.7 fusion.260
  372.4 1.9 and_convert_fusion.4
  376.5 2.4 multiply_multiply_fusion.8
  382.3 40.7 %custom-call.11 = f32[8,1,64,64]{2,3,1,0:T(8,128)} custom-call(f32[8,1,64,64]{3,2,1,0:T(8,128)} %fusion.259), custom_call_target="InvertDiagBlocksLowerTriangular" | custom-call | tf_op jit(solution)/shard_map/while/body/eval_jaxpr/jit(_solve_triangular)/vmap()/triangular_solve | solution.py:154
  423.0 1.7 fusion.260
  441.2 1.9 and_convert_fusion.4
  445.2 2.4 multiply_multiply_fusion.8
  451.0 40.7 %custom-call.11 = f32[8,1,64,64]{2,3,1,0:T(8,128)} custom-call(f32[8,1,64,64]{3,2,1,0:T(8,128)} %fusion.259), custom_call_target="InvertDiagBlocksLowerTriangular" | custom-call | tf_op jit(solution)/shard_map/while/body/eval_jaxpr/jit(_solve_triangular)/vmap()/triangular_solve | solution.py:154
  503.7 2.4 copy.127
  506.1 2.4 slice_bitcast_fusion.1
  508.5 2.1 fusion.152
  510.6 2.8 copy.135
  513.5 55.6 %while.28 = (s32[]{:T(128)}, f32[8,64,64]{2,1,0:T(8,128)S(1)}, f32[8,64,64]{2,1,0:T(8,128)S(1)}, f32[8,64,64]{2,1,0:T(8,128)S(1)}, s32[]{:T(128)}, /*index=5*/s32[]{:T(128)}) while((s32[]{:T(128)}, f32[8,64,64]{2,1,0:T(8,128)S(1)}, f32[8,64,64]{2,1,0:T(8,128)S(1)}, f32[8,64,64]{2,1,0:T(8,128)S(1)}, s32[]{:T(128)}, ...), condition=%wide.region_9.10_spmd.clone, body=%wide.region_8.9_spmd.clone.sunk | while | flops 25296900 | bytes 917623 | solution.py:213
  513.9 3.4 collective-permute-start
  517.3 2.5 collective-permute-done
  520.2 4.4 collective-permute-start
  524.6 2.5 collective-permute-done
  527.5 4.4 collective-permute-start
  531.9 2.5 collective-permute-done
  534.8 5.2 collective-permute-start
  540.1 2.5 collective-permute-done
  543.0 5.3 collective-permute-start
  548.3 3.3 collective-permute-done
  552.0 5.5 collective-permute-start
  557.5 3.3 collective-permute-done
  561.3 5.0 collective-permute-start
  566.3 2.5 collective-permute-done
  569.1 4.1 fusion.157
  576.0 4.4 fusion.116
  582.6 4.0 convolution_convert_fusion
  589.5 22.9 %all-reduce.2 = (bf16[1,512]{1,0:T(2,128)(2,1)S(1)}, bf16[1,512]{1,0:T(2,128)(2,1)S(1)}) all-reduce(bf16[1,512]{1,0:T(2,128)(2,1)S(1)} %get-tuple-element.333, bf16[1,512]{1,0:T(2,128)(2,1)S(1)} %get-tuple-element.332), channel_id=1, replica_groups=mesh['seq'=8,'tp'=4] {'seq'}, use_global_device_ids=true, to_apply=%region_16.17 | all-reduce | flops 1024 | bytes 4096 | tf_op jit(solution)/shard_map/psum | solution.py:30
  613.0 44.5 %all-reduce.6.cloned.1.call-done = (bf16[8,64,64]{2,1,0:T(8,128)(2,1)}, bf16[8,64,64]{2,1,0:T(8,128)(2,1)}) async-done(((bf16[8,64,64]{2,1,0:T(8,128)(2,1)}, bf16[8,64,64]{2,1,0:T(8,128)(2,1)}), (bf16[8,64,64]{2,1,0:T(8,128)(2,1)}, bf16[8,64,64]{2,1,0:T(8,128)(2,1)})) %all-reduce.6.cloned.1.call-update) | async-done | bytes 131088 | tf_op jit(solution)/shard_map/psum | solution.py:30
  657.5 1.7 select_bitcast_fusion
  659.2 1.8 add_convert_fusion
  (345 shorter events, 138.3 us)
Async XLA Ops:
  8.0 50.0 %copy-start = (bf16[2048,512]{1,0:T(8,128)(2,1)S(1)}, bf16[2048,512]{1,0:T(8,128)(2,1)}, u32[]{:S(2)}) copy-start(bf16[2048,512]{1,0:T(8,128)(2,1)} %param.33) | copy-start | bytes 6291460
  8.0 23.9 %copy-start.7 = (bf16[384,512]{1,0:T(8,128)(2,1)S(1)}, bf16[384,512]{1,0:T(8,128)(2,1)}, u32[]{:S(2)}) copy-start(bf16[384,512]{1,0:T(8,128)(2,1)} %param.26) | copy-start | bytes 1179652
  8.0 649.5 %all-reduce.6.cloned.1.call-start = ((), (), s32[]{:S(2)}) async-start(), calls=%async_computation.2 | async-start | bytes 524288 | tf_op jit(solution)/shard_map/psum | solution.py:30
  8.1 8.1 %collective-permute-start.1 = (bf16[384,512]{1,0:T(8,128)(2,1)}, bf16[384,512]{1,0:T(8,128)(2,1)S(1)}, u32[]{:S(2)}, u32[]{:S(2)}) collective-permute-start(bf16[384,512]{1,0:T(8,128)(2,1)} %param.26), channel_id=1, source_target_pairs={{0,1},{1,2},{2,3},{3,0},{4,5},{5,6},{6,7},{7,4},{8,9},{9,10},{10,1... | collective-permute-start | bytes 1179656 | tf_op jit(solution)/shard_map/ppermute | solution.py:16
  16.2 7.2 %collective-permute-start.2 = (bf16[384,512]{1,0:T(8,128)(2,1)S(1)}, bf16[384,512]{1,0:T(8,128)(2,1)S(1)}, u32[]{:S(2)}, u32[]{:S(2)}) collective-permute-start(bf16[384,512]{1,0:T(8,128)(2,1)S(1)} %collective-permute-done.1), channel_id=1, source_target_pairs={{0,1},{1,2},{2,3},{3,0},{4,5},{5,6},{6,7},{7,4},{8,9},{9,10},{10,1... | collective-permute-start | bytes 1179656 | tf_op jit(solution)/shard_map/ppermute | solution.py:16
  23.4 7.2 %collective-permute-start.3 = (bf16[384,512]{1,0:T(8,128)(2,1)S(1)}, bf16[384,512]{1,0:T(8,128)(2,1)S(1)}, u32[]{:S(2)}, u32[]{:S(2)}) collective-permute-start(bf16[384,512]{1,0:T(8,128)(2,1)S(1)} %collective-permute-done.2), channel_id=1, source_target_pairs={{0,1},{1,2},{2,3},{3,0},{4,5},{5,6},{6,7},{7,4},{8,9},{9,10},{10,1... | collective-permute-start | bytes 1179656 | tf_op jit(solution)/shard_map/ppermute | solution.py:16
  31.8 1.1 copy-start.16
  32.0 9.2 %copy-start.17 = (f32[512]{0:T(512)S(1)}, f32[512]{0:T(512)}, u32[]{:S(2)}) copy-start(f32[512]{0:T(512)} %param.46) | copy-start | bytes 6148
  32.0 9.2 %copy-start.18 = (f32[512]{0:T(512)S(1)}, f32[512]{0:T(512)}, u32[]{:S(2)}) copy-start(f32[512]{0:T(512)} %param.47) | copy-start | bytes 6148
  33.4 1.2 copy-start.4
  34.6 10.3 %collective-permute-start.4 = (bf16[1,2048]{1,0:T(2,128)(2,1)S(1)}, bf16[1,2048]{1,0:T(2,128)(2,1)S(1)}, u32[]{:S(2)}, u32[]{:S(2)}) collective-permute-start(bf16[1,2048]{1,0:T(2,128)(2,1)S(1)} %slice.132), channel_id=1, source_target_pairs={{0,4},{4,8},{8,12},{12,16},{16,20},{20,24},{24,28},{1,5},{5,9},{9,... | collective-permute-start | bytes 12296 | tf_op jit(solution)/shard_map/ppermute | solution.py:25
  39.1 18.9 %copy-start.27 = (pred[384]{0:T(512)(128)(4,1)}, pred[384]{0:T(512)(128)(4,1)S(1)}, u32[]{:S(2)}) copy-start(pred[384]{0:T(512)(128)(4,1)S(1)} %pad_add_fusion) | copy-start | bytes 1156
  41.5 3.5 copy-start.20
  41.5 3.5 copy-start.22
  50.4 7.6 %copy-start.23 = (f32[512]{0:T(512)S(1)}, f32[512]{0:T(512)}, u32[]{:S(2)}) copy-start(f32[512]{0:T(512)} %param.44) | copy-start | bytes 6148
  50.4 7.6 %copy-start.24 = (f32[512]{0:T(512)S(1)}, f32[512]{0:T(512)}, u32[]{:S(2)}) copy-start(f32[512]{0:T(512)} %param.45) | copy-start | bytes 6148
  63.5 4.0 copy-start.21
  63.5 4.0 copy-start.25
  63.5 4.0 copy-start.28
  72.6 5.3 copy-start.14
  83.9 6.1 copy-start.10
  85.6 2.8 copy-start.6
  85.6 5.4 copy-start.26
  85.6 5.4 copy-start.30
  148.0 4.9 copy-start.1
  153.9 2.8 copy-start.2
  216.7 4.9 copy-start.1
  222.6 2.8 copy-start.2
  285.5 4.9 copy-start.1
  291.4 2.8 copy-start.2
  354.2 4.9 copy-start.1
  360.1 2.8 copy-start.2
  423.0 4.9 copy-start.1
  428.9 2.8 copy-start.2
  491.7 4.9 copy-start.1
  497.6 2.8 copy-start.2
  506.1 2.4 copy-start.5
  508.5 5.0 copy-start.3
  513.9 5.9 collective-permute-start
  520.2 6.9 %collective-permute-start = (bf16[8,64,64]{2,1,0:T(8,128)(2,1)S(1)}, bf16[8,64,64]{2,1,0:T(8,128)(2,1)S(1)}, u32[]{:S(2)}, u32[]{:S(2)}) collective-permute-start(bf16[8,64,64]{2,1,0:T(8,128)(2,1)S(1)} %fusion.267), channel_id=1, source_target_pairs={{0,4},{4,8},{8,12},{12,16},{16,20},{20,24},{24,28},{1,5},{5,9},{9,... | collective-permute-start | bytes 196616 | tf_op jit(solution)/shard_map/while/body/eval_jaxpr/ppermute | solution.py:25
  527.5 6.9 %collective-permute-start = (bf16[8,64,64]{2,1,0:T(8,128)(2,1)S(1)}, bf16[8,64,64]{2,1,0:T(8,128)(2,1)S(1)}, u32[]{:S(2)}, u32[]{:S(2)}) collective-permute-start(bf16[8,64,64]{2,1,0:T(8,128)(2,1)S(1)} %fusion.267), channel_id=1, source_target_pairs={{0,4},{4,8},{8,12},{12,16},{16,20},{20,24},{24,28},{1,5},{5,9},{9,... | collective-permute-start | bytes 196616 | tf_op jit(solution)/shard_map/while/body/eval_jaxpr/ppermute | solution.py:25
  534.8 7.7 %collective-permute-start = (bf16[8,64,64]{2,1,0:T(8,128)(2,1)S(1)}, bf16[8,64,64]{2,1,0:T(8,128)(2,1)S(1)}, u32[]{:S(2)}, u32[]{:S(2)}) collective-permute-start(bf16[8,64,64]{2,1,0:T(8,128)(2,1)S(1)} %fusion.267), channel_id=1, source_target_pairs={{0,4},{4,8},{8,12},{12,16},{16,20},{20,24},{24,28},{1,5},{5,9},{9,... | collective-permute-start | bytes 196616 | tf_op jit(solution)/shard_map/while/body/eval_jaxpr/ppermute | solution.py:25
  543.0 8.6 %collective-permute-start = (bf16[8,64,64]{2,1,0:T(8,128)(2,1)S(1)}, bf16[8,64,64]{2,1,0:T(8,128)(2,1)S(1)}, u32[]{:S(2)}, u32[]{:S(2)}) collective-permute-start(bf16[8,64,64]{2,1,0:T(8,128)(2,1)S(1)} %fusion.267), channel_id=1, source_target_pairs={{0,4},{4,8},{8,12},{12,16},{16,20},{20,24},{24,28},{1,5},{5,9},{9,... | collective-permute-start | bytes 196616 | tf_op jit(solution)/shard_map/while/body/eval_jaxpr/ppermute | solution.py:25
  552.0 8.9 %collective-permute-start = (bf16[8,64,64]{2,1,0:T(8,128)(2,1)S(1)}, bf16[8,64,64]{2,1,0:T(8,128)(2,1)S(1)}, u32[]{:S(2)}, u32[]{:S(2)}) collective-permute-start(bf16[8,64,64]{2,1,0:T(8,128)(2,1)S(1)} %fusion.267), channel_id=1, source_target_pairs={{0,4},{4,8},{8,12},{12,16},{16,20},{20,24},{24,28},{1,5},{5,9},{9,... | collective-permute-start | bytes 196616 | tf_op jit(solution)/shard_map/while/body/eval_jaxpr/ppermute | solution.py:25
  561.3 7.5 %collective-permute-start = (bf16[8,64,64]{2,1,0:T(8,128)(2,1)S(1)}, bf16[8,64,64]{2,1,0:T(8,128)(2,1)S(1)}, u32[]{:S(2)}, u32[]{:S(2)}) collective-permute-start(bf16[8,64,64]{2,1,0:T(8,128)(2,1)S(1)} %fusion.267), channel_id=1, source_target_pairs={{0,4},{4,8},{8,12},{12,16},{16,20},{20,24},{24,28},{1,5},{5,9},{9,... | collective-permute-start | bytes 196616 | tf_op jit(solution)/shard_map/while/body/eval_jaxpr/ppermute | solution.py:25
  569.1 4.3 copy-start.9
  569.1 4.3 copy-start.11
  573.2 2.7 copy-start.29
  576.0 4.5 copy-start.13
  576.0 5.5 copy-start.12
  576.0 6.6 copy-start.15
  582.5 4.2 copy-start.19
  582.6 76.6 %copy-start.8 = (bf16[384,512]{1,0:T(8,128)(2,1)S(1)}, bf16[384,512]{1,0:T(8,128)(2,1)}, u32[]{:S(2)}) copy-start(bf16[384,512]{1,0:T(8,128)(2,1)} %param.26) | copy-start | bytes 1179652
  582.6 76.6 %reduce-scatter.2.cloned.1.call-start = ((), (), s32[]{:S(2)}) async-start(), calls=%async_computation.1 | async-start | bytes 1966080 | tf_op jit(solution)/shard_map/reduce_scatter | solution.py:239
Sparse Core Ops, SparseCore 0:
  582.7 74.7 all-reduce.5
Sparse Core Ops, SparseCore 1:
  586.8 32.0 reduce-scatter.1
